TPU v7x, 256 devices: a whole 4x4x8 slice. The times are simulated.
256 devices in a mesh: dp: 32 (over y, z), vocab: 8 (over x, core).
Axes of the slice: x: 4, y: 4, z: 8, core: 2. Of those that a mesh axis runs over, the one named last changes fastest.
Arguments:
- hidden: bfloat16 [12288, 4096], P('dp'), may hold values from -6 to 6
- head_weight: bfloat16 [4096, 16000], P('dp', 'vocab'), may hold values from -0.09375 to 0.09375
- head_bias: float32 [16000], P('vocab'), may hold values from -3.5 to -1.5
- query_len: int32 [128], P('dp'), may hold values from 8 to 32
- passage_len: int32 [128], P('dp'), may hold values from 16 to 64
- neg_owner: int32 [128, 8], P('dp'), may hold values from 0 to 31, all different within a row; in each aligned block of 4 rows (0 to 3, 4 to 7, ...) at most 2 rows name the same one
- neg_index: int32 [128, 8], P('dp'), may hold values from 0 to 3
- teacher: float32 [128, 8], P('dp'), may hold values from -8 to 8
Outputs:
- margin_error: float32 [128, 8], P('dp')
- hidden_grad: float32 [12288, 4096], P(('dp', 'vocab'))
Inputs may be any that keep to these rules, and one draw needn't show every extreme that they name: `neg_owner`: the 8 negatives of a query have different holders. Among the queries of one index of dp no holder appears more than 2 times, and in some of those blocks one holder appears exactly 2 times.
All inputs are finite; a program needn't handle non-finite values.
Results may differ from a plain program's by a relative error of at most 0.0028.
Values may be sent and summed in bfloat16 or wider, within the bound.
A program may use at most 128 MiB of HBM per device.

v0:
```python
import jax
import jax.numpy as jnp
from jax import lax
from jax.sharding import PartitionSpec as P

LQ = 32
LP = 64
TAU = 0.05


def soft_pool(token_logits, token_mask):
    activation = jnp.log1p(jnp.maximum(token_logits, 0.0))
    weights = jnp.exp(activation / TAU) * token_mask[:, :, None]
    summed = jnp.sum(weights, axis=1)
    valid_count = jnp.sum(token_mask, axis=1)[:, None]
    return (TAU * jnp.log(summed / valid_count), weights / summed[:, None, :])


def lengths_mask(lengths, span):
    return (jnp.arange(span)[None, :] < lengths[:, None]).astype(jnp.float32)


def per_device(
    hidden, head_weight, head_bias, query_len, passage_len, neg_owner, neg_index, teacher
):
    query_count = neg_owner.shape[0]
    neg_count = neg_owner.shape[1]
    owners = lax.axis_size("dp")
    head_full = lax.all_gather(head_weight, "dp", axis=0, tiled=True)
    vocab_width = head_full.shape[1]
    logits = jnp.dot(hidden, head_full, preferred_element_type=jnp.float32) + head_bias[None, :]
    query_tokens = query_count * LQ
    query_rep, query_weights = soft_pool(
        logits[:query_tokens].reshape(query_count, LQ, vocab_width), lengths_mask(query_len, LQ)
    )
    passage_rep, passage_weights = soft_pool(
        logits[query_tokens:].reshape(query_count, LP, vocab_width), lengths_mask(passage_len, LP)
    )
    gathered = lax.all_gather(passage_rep, "dp", axis=0, tiled=True)
    passage_ids = neg_owner * query_count + neg_index
    neg_rows = jnp.take(gathered, passage_ids.reshape(-1), axis=0).reshape(
        query_count, neg_count, vocab_width
    )
    pos_part = jnp.sum(query_rep * passage_rep, axis=1)
    neg_part = jnp.sum(query_rep[:, None, :] * neg_rows, axis=2)
    positive, negative = lax.psum((pos_part, neg_part), "vocab")
    margin_error = positive[:, None] - negative - teacher
    grad_pos = jnp.sum(margin_error, axis=1)
    grad_neg = -margin_error
    query_grad = grad_pos[:, None] * passage_rep + jnp.sum(grad_neg[:, :, None] * neg_rows, axis=1)
    neg_terms = (grad_neg[:, :, None] * query_rep[:, None, :]).reshape(-1, vocab_width)
    scattered = jax.ops.segment_sum(
        neg_terms, passage_ids.reshape(-1), num_segments=owners * query_count
    )
    returned_grad = lax.psum_scatter(scattered, "dp", scatter_dimension=0, tiled=True)
    passage_grad = grad_pos[:, None] * query_rep + returned_grad
    relu_slope = (logits > 0).astype(jnp.float32) / (1.0 + jnp.maximum(logits, 0.0))
    d_query = (query_grad[:, None, :] * query_weights).reshape(-1, vocab_width)
    d_passage = (passage_grad[:, None, :] * passage_weights).reshape(-1, vocab_width)
    logit_grad = (jnp.concatenate([d_query, d_passage], axis=0) * relu_slope).astype(jnp.bfloat16)
    hidden_grad = lax.psum_scatter(
        lax.dot_general(
            logit_grad, head_full, (((1,), (1,)), ((), ())), preferred_element_type=jnp.float32
        ),
        "vocab",
        scatter_dimension=0,
        tiled=True,
    )
    return (margin_error, hidden_grad)


def solution(mesh):
    return jax.shard_map(
        per_device,
        mesh=mesh,
        in_specs=(
            P("dp", None),
            P("dp", "vocab"),
            P("vocab"),
            P("dp"),
            P("dp"),
            P("dp", None),
            P("dp", None),
            P("dp", None),
        ),
        out_specs=(P("dp", None), P(("dp", "vocab"), None)),
        check_vma=False,
    )
```

profile of v0, /device:TPU:1, one launch (start us, length us, event | category | flops | bytes accessed | tf_op | source)
XLA Modules:
  0.0 486.5 jit_solution(886235719207810661)
XLA Ops:
  8.0 0.9 compare_and_fusion
  11.0 0.8 fusion.21
  13.3 144.3 %all-gather.3.cloned.1.call-done = bf16[4096,2000]{0,1:T(8,128)(2,1)} async-done(((bf16[128,2000]{0,1:T(8,128)(2,1)}), bf16[4096,2000]{0,1:T(8,128)(2,1)}) %all-gather.3.cloned.1.call-update) | async-done | bytes 16384016 | tf_op jit(solution)/shard_map/all_gather | solution.py:29
  157.6 12.0 %convolution_add_fusion = f32[384,2000]{0,1:T(8,128)S(1)} fusion(bf16[384,4096]{1,0:T(8,128)(2,1)S(1)} %copy-done, bf16[4096,2000]{0,1:T(8,128)(2,1)} %all-gather.3.cloned.1.call-done, f32[2000]{0:T(1024)} %param.10), kind=kOutput, calls=%fused_computation.4 | convolution fusion | flops 6292224000 | bytes 22609728 | tf_op jit(solution)/shard_map/dot_general | solution.py:31
  169.6 1.7 fusion.10
  171.5 2.2 fusion.3
  173.7 2.6 copy.18
  176.3 2.9 copy.19
  179.2 1.4 multiply_reduce_fusion.1
  180.6 1.9 multiply_reduce_fusion
  183.3 42.1 %all-gather = f32[32,4,2000]{2,1,0:T(4,128)} all-gather(f32[1,4,2000]{2,1,0:T(4,128)S(1)} %multiply_bitcast_fusion), channel_id=1, replica_groups=mesh['dp'=32,'vocab'=8] {'dp'}, dimensions={0}, use_global_device_ids=true | all-gather | bytes 1056000 | tf_op jit(solution)/shard_map/all_gather | solution.py:39
  225.4 2.6 reshape.212
  228.0 2.0 gather_fusion
  230.0 1.5 fusion.13
  232.2 27.3 %all-reduce.1 = (f32[4,8]{1,0:T(4,128)}, f32[4]{0:T(128)}) all-reduce(f32[4,8]{1,0:T(4,128)S(1)} %reduce_sum.80, f32[4]{0:T(128)S(1)} %get-tuple-element.6), channel_id=1, replica_groups=mesh['dp'=32,'vocab'=8] {'vocab'}, use_global_device_ids=true, to_apply=%region_7.8 | all-reduce | flops 36 | bytes 288 | tf_op jit(solution)/shard_map/psum | solution.py:46
  259.4 1.5 fusion.26
  261.6 2.2 scatter_custom_fusion
  264.8 1.3 dynamic-slice
  266.7 1.1 div.69
  267.8 2.6 copy.20
  270.4 1.7 div.72
  272.1 3.0 copy.23
  275.2 130.2 %all-reduce.4.cloned.1.call-done = f32[128,2000]{1,0:T(8,128)} async-done(((f32[128,2000]{1,0:T(8,128)}), f32[128,2000]{1,0:T(8,128)}) %all-reduce.4.cloned.1.call-update) | async-done | bytes 1024016
  405.4 0.9 multiply_add_fusion
  406.3 1.1 mul.145
  407.4 2.6 copy.21
  410.1 1.6 mul.154
  411.7 2.9 copy.24
  414.6 2.6 divide_multiply_fusion.1
  417.4 3.3 divide_multiply_fusion
  420.7 12.6 %fusion.4 = f32[384,4096]{1,0:T(8,128)} fusion(bf16[4096,2000]{0,1:T(8,128)(2,1)} %all-gather.3.cloned.1.call-done, f32[256,2000]{0,1:T(8,128)S(1)} %divide_multiply_fusion, f32[128,2000]{0,1:T(8,128)S(1)} %divide_multiply_fusion.1, f32[384,2000]{0,1:T(8,128)S(1)} %copy-done.2), kind=kOutput, calls=%fused_computation.11 | convolution fusion | flops 6297600000 | bytes 28819456 | tf_op jit(solution)/shard_map/dot_general | solution.py:62
  433.4 46.6 %reduce-scatter.2.cloned.1.call-done = f32[48,4096]{1,0:T(8,128)} async-done(((f32[384,4096]{1,0:T(8,128)}), f32[48,4096]{1,0:T(8,128)}) %reduce-scatter.2.cloned.1.call-update) | async-done | bytes 786448 | tf_op jit(solution)/shard_map/reduce_scatter | solution.py:61
  (44 shorter events, 8.3 us)
Async XLA Ops:
  7.2 150.4 %copy-start = (bf16[384,4096]{1,0:T(8,128)(2,1)S(1)}, bf16[384,4096]{1,0:T(8,128)(2,1)}, u32[]{:S(2)}) copy-start(bf16[384,4096]{1,0:T(8,128)(2,1)} %param.8) | copy-start | bytes 9437188
  7.2 150.4 %all-gather.3.cloned.1.call-start = ((), (), s32[]{:S(2)}) async-start(), calls=%async_computation.1 | async-start | bytes 16896000 | tf_op jit(solution)/shard_map/all_gather | solution.py:29
  7.9 397.5 %all-reduce.4.cloned.1.call-start = ((), (), s32[]{:S(2)}) async-start(), calls=%async_computation.3 | async-start | bytes 2097152
  8.8 160.8 %copy-start.7 = (pred[4,8]{1,0:T(4,128)(4,1)}, pred[4,8]{1,0:T(4,128)(4,1)S(1)}, u32[]{:S(2)}) copy-start(pred[4,8]{1,0:T(4,128)(4,1)S(1)} %get-tuple-element.9) | copy-start | bytes 100
  169.6 1.9 copy-start.1
  182.7 0.6 copy-start.3
  260.9 9.5 %copy-start.5 = (f32[4,8]{1,0:T(4,128)}, f32[4,8]{1,0:T(4,128)S(1)}, u32[]{:S(2)}) copy-start(f32[4,8]{1,0:T(4,128)S(1)} %get-tuple-element.5) | copy-start | bytes 388
  263.8 216.2 %reduce-scatter.2.cloned.1.call-start = ((), (), s32[]{:S(2)}) async-start(), calls=%async_computation.2 | async-start | bytes 7077888 | tf_op jit(solution)/shard_map/reduce_scatter | solution.py:61
  272.1 3.0 copy-start.8
  272.1 3.1 copy-start.9
  272.1 133.3 %copy-start.4 = (f32[4,2000]{1,0:T(4,128)S(1)}, f32[4,2000]{1,0:T(4,128)}, u32[]{:S(2)}) copy-start(f32[4,2000]{1,0:T(4,128)} %copy-done.3) | copy-start | bytes 96004
  411.7 2.9 copy-start.6
  414.6 2.8 copy-start.2
Sparse Core Ops, SparseCore 0:
  10.5 147.1 all-gather.2
  263.9 141.4 all-reduce.3
  433.5 46.4 reduce-scatter.1
where the time goes:
time: 487 us
  waiting for transfers between devices  322 us (66%)
  blocking collectives  69.3 us (14%)
  local copies, waits for them, and re-layouts  32.5 us (7%)
  matrix products  24.6 us (5%)
  other arithmetic  23.6 us (5%)
  between operations  14.5 us (3%)
    all_gather x1, waiting for transfers between devices, per_device(): head_full = lax.all_gather(head_weight, 'dp', axis=0, tiled=True)  144 us
    unnamed x4, waiting for transfers between devices  131 us
    reduce_scatter x1, waiting for transfers between devices, per_device(): lax.psum_scatter(lax.dot_general(logit_grad, head_full, (((1,), (1,)), ((...  46.6 us
    all_gather x1, blocking collectives, per_device(): gathered = lax.all_gather(passage_rep, 'dp', axis=0, tiled=True)  42.1 us
    psum x1, blocking collectives, per_device(): positive, negative = lax.psum((pos_part, neg_part), 'vocab')  27.3 us
    dot_general x1, matrix products, per_device(): lax.dot_general(logit_grad, head_full, (((1,), (1,)), ((), ())), preferre...  12.6 us
    dot_general x1, matrix products, per_device(): jnp.dot(hidden, head_full, preferred_element_type=jnp.float32)  12 us
  transfers between devices with their start and end apart: 3, of which 3 were waited for; matrix products, arithmetic and copies ran while one was open for 3% of the time, Pallas kernels for 0%

commit v1 on v0

--- a/solution.py
+++ b/solution.py
@@ -6,6 +6,13 @@
 LQ = 32
 LP = 64
 TAU = 0.05
+
+
+def raise_the_outputs(patch, group_axis, pos_dim):
+    return jnp.concatenate(
+        lax.all_to_all(jnp.stack([patch] * lax.axis_size(group_axis), axis=0), group_axis, 0, 0),
+        axis=pos_dim,
+    )
 
 
 def soft_pool(token_logits, token_mask):
@@ -26,7 +33,7 @@
     query_count = neg_owner.shape[0]
     neg_count = neg_owner.shape[1]
     owners = lax.axis_size("dp")
-    head_full = lax.all_gather(head_weight, "dp", axis=0, tiled=True)
+    head_full = raise_the_outputs(head_weight, "dp", 0)
     vocab_width = head_full.shape[1]
     logits = jnp.dot(hidden, head_full, preferred_element_type=jnp.float32) + head_bias[None, :]
     query_tokens = query_count * LQ

time: 487 us -> 749 us (1.54)
  waiting for transfers between devices: 322 us -> 563 us
  local copies, waits for them, and re-layouts: 32.5 us -> 45.6 us
  starting transfers between devices: 0.3 us -> 12.5 us
  other arithmetic: 23.6 us -> 11.8 us
    all_to_all x0 -> x1, waiting for transfers between devices: none -> 379 us  [raise_the_outputs(): lax.all_to_all(jnp.stack([patch] * lax.axis_size(group_axis), axis=0), gr...]
    all_gather x1 -> x0, waiting for transfers between devices: 144 us -> none  [per_device(): head_full = lax.all_gather(head_weight, 'dp', axis=0, tiled=True)]
    all_to_all x0 -> x1, local copies, waits for them, and re-layouts: none -> 22.6 us  [raise_the_outputs(): lax.all_to_all(jnp.stack([patch] * lax.axis_size(group_axis), axis=0), gr...]
    all_to_all x0 -> x1, starting transfers between devices: none -> 12.3 us  [raise_the_outputs(): lax.all_to_all(jnp.stack([patch] * lax.axis_size(group_axis), axis=0), gr...]
    all_gather x1, blocking collectives: 42.1 us -> 52.2 us  [per_device(): gathered = lax.all_gather(passage_rep, 'dp', axis=0, tiled=True)]
    unnamed x4 -> x3, waiting for transfers between devices: 131 us -> 137 us
  transfers between devices with their start and end apart: 3 -> 3, of which waited for: 3 -> 3; matrix products, arithmetic and copies ran while one was open for 3% -> 1% of each run, Pallas kernels for 0% -> 0%
where the time goes in v1:
time: 749 us; the launch traced here: 748 us
  waiting for transfers between devices  563 us (75%)
  blocking collectives  76.3 us (10%)
  local copies, waits for them, and re-layouts  45.6 us (6%)
  matrix products  24.5 us (3%)
  between operations  14.9 us (2%)
  starting transfers between devices  12.5 us (2%)
  other arithmetic  11.8 us (2%)
    all_to_all x1, waiting for transfers between devices, raise_the_outputs(): lax.all_to_all(jnp.stack([patch] * lax.axis_size(group_axis), axis=0), gr...  379 us
    unnamed x3, waiting for transfers between devices  137 us
    all_gather x1, blocking collectives, per_device(): gathered = lax.all_gather(passage_rep, 'dp', axis=0, tiled=True)  52.2 us
    reduce_scatter x1, waiting for transfers between devices, per_device(): lax.psum_scatter(lax.dot_general(logit_grad, head_full, (((1,), (1,)), ((...  46.7 us
    psum x1, blocking collectives, per_device(): positive, negative = lax.psum((pos_part, neg_part), 'vocab')  24.1 us
    all_to_all x1, local copies, waits for them, and re-layouts, raise_the_outputs(): lax.all_to_all(jnp.stack([patch] * lax.axis_size(group_axis), axis=0), gr...  22.6 us
  transfers between devices with their start and end apart: 3, of which 3 were waited for; matrix products, arithmetic and copies ran while one was open for 1% of the time, Pallas kernels for 0%

profile of v1, /device:TPU:1, one launch (start us, length us, event | category | flops | bytes accessed | tf_op | source)
XLA Modules:
  0.0 748.5 jit_solution(14651119828422621183)
XLA Ops:
  7.2 7.3 stack.2
  14.5 12.3 %all-to-all-start = ((bf16[32,128,2000]{1,2,0:T(8,128)(2,1)}), bf16[32,128,2000]{1,2,0:T(8,128)(2,1)}, u32[]{:S(2)}, u32[]{:S(2)}) async-start(bf16[32,128,2000]{1,2,0:T(8,128)(2,1)} %stack.2), calls=%async_computation | async-start | bytes 32768000 | tf_op jit(solution)/shard_map/all_to_all | solution.py:13
  27.6 378.6 %all-to-all-done = bf16[32,128,2000]{1,2,0:T(8,128)(2,1)} async-done(((bf16[32,128,2000]{1,2,0:T(8,128)(2,1)}), bf16[32,128,2000]{1,2,0:T(8,128)(2,1)}, u32[]{:S(2)}, u32[]{:S(2)}) %all-to-all-start) | async-done | bytes 16384032 | tf_op jit(solution)/shard_map/all_to_all | solution.py:13
  406.2 22.6 %copy.27 = bf16[32,128,2000]{2,1,0:T(8,128)(2,1)} copy(bf16[32,128,2000]{1,2,0:T(8,128)(2,1)} %all-to-all-done) | data formatting | bytes 32768000 | tf_op jit(solution)/shard_map/all_to_all | solution.py:13
  428.9 12.2 %convolution_add_fusion = f32[384,2000]{0,1:T(8,128)S(1)} fusion(bf16[384,4096]{1,0:T(8,128)(2,1)S(1)} %copy-done, bf16[4096,2000]{1,0:T(8,128)(2,1)} %bitcast.29, f32[2000]{0:T(1024)S(1)} %copy-done.12), kind=kOutput, calls=%fused_computation.4 | convolution fusion | flops 6292224000 | bytes 22609728 | tf_op jit(solution)/shard_map/dot_general | solution.py:38
  441.1 2.2 fusion.3
  443.4 1.4 fusion.10
  444.8 1.9 copy.29
  446.7 1.5 copy.28
  448.2 0.3 multiply_reduce_fusion
  448.8 0.2 multiply_reduce_fusion.2
  449.0 52.2 %all-gather = f32[32,4,2000]{2,1,0:T(4,128)S(1)} all-gather(f32[1,4,2000]{2,1,0:T(4,128)S(1)} %multiply_bitcast_fusion), channel_id=1, replica_groups=mesh['dp'=32,'vocab'=8] {'dp'}, dimensions={0}, use_global_device_ids=true | all-gather | bytes 1056000 | tf_op jit(solution)/shard_map/all_gather | solution.py:46
  501.2 0.4 reshape.218
  501.6 0.7 gather_fusion
  502.2 0.2 fusion.13
  502.5 24.1 %all-reduce.1 = (f32[4,8]{1,0:T(4,128)S(1)}, f32[4]{0:T(128)S(1)}) all-reduce(f32[4,8]{1,0:T(4,128)S(1)} %reduce_sum.80, f32[4]{0:T(128)S(1)} %get-tuple-element.6), channel_id=1, replica_groups=mesh['dp'=32,'vocab'=8] {'vocab'}, use_global_device_ids=true, to_apply=%region_7.8 | all-reduce | flops 36 | bytes 288 | tf_op jit(solution)/shard_map/psum | solution.py:53
  526.9 2.0 scatter_custom_fusion
  529.0 0.2 reduce-scatter.2.cloned.1.call-start
  529.4 0.6 dynamic-slice
  530.7 1.3 copy.30
  532.0 0.2 div.72
  532.3 1.8 copy.33
  534.3 137.5 %all-reduce.4.cloned.1.call-done = f32[128,2000]{1,0:T(8,128)} async-done(((f32[128,2000]{1,0:T(8,128)}), f32[128,2000]{1,0:T(8,128)}) %all-reduce.4.cloned.1.call-update) | async-done | bytes 1024016
  671.7 0.9 multiply_add_fusion
  672.7 1.3 copy.31
  674.0 1.6 mul.154
  675.6 3.0 copy.34
  678.7 2.2 divide_multiply_fusion.1
  680.9 0.5 copy-done.5
  681.5 1.1 divide_multiply_fusion
  682.6 12.3 %fusion.4 = f32[384,4096]{1,0:T(8,128)} fusion(bf16[4096,2000]{1,0:T(8,128)(2,1)} %bitcast.30, f32[256,2000]{0,1:T(8,128)S(1)} %divide_multiply_fusion, f32[128,2000]{0,1:T(8,128)S(1)} %divide_multiply_fusion.1, f32[384,2000]{0,1:T(8,128)S(1)} %copy-done.3), kind=kOutput, calls=%fused_computation.11 | convolution fusion | flops 6297600000 | bytes 28819456 | tf_op jit(solution)/shard_map/dot_general | solution.py:69
  694.9 46.7 %reduce-scatter.2.cloned.1.call-done = f32[48,4096]{1,0:T(8,128)} async-done(((f32[384,4096]{1,0:T(8,128)}), f32[48,4096]{1,0:T(8,128)}) %reduce-scatter.2.cloned.1.call-update) | async-done | bytes 786448 | tf_op jit(solution)/shard_map/reduce_scatter | solution.py:68
  (53 shorter events, 2.0 us)
Async XLA Ops:
  7.2 421.7 %copy-start = (bf16[384,4096]{1,0:T(8,128)(2,1)S(1)}, bf16[384,4096]{1,0:T(8,128)(2,1)}, u32[]{:S(2)}) copy-start(bf16[384,4096]{1,0:T(8,128)(2,1)} %param.8) | copy-start | bytes 9437188
  14.4 12.4 %copy-start.8 = (s32[4,8]{1,0:T(4,128)S(1)}, s32[4,8]{1,0:T(4,128)}, u32[]{:S(2)}) copy-start(s32[4,8]{1,0:T(4,128)} %param.14) | copy-start | bytes 388
  14.4 12.4 %copy-start.9 = (s32[4,8]{1,0:T(4,128)S(1)}, s32[4,8]{1,0:T(4,128)}, u32[]{:S(2)}) copy-start(s32[4,8]{1,0:T(4,128)} %param.13) | copy-start | bytes 388
  14.4 12.7 %copy-start.10 = (s32[4]{0:T(128)S(1)}, s32[4]{0:T(128)}, u32[]{:S(2)}) copy-start(s32[4]{0:T(128)} %param.12) | copy-start | bytes 52
  14.4 12.9 %copy-start.11 = (s32[4]{0:T(128)S(1)}, s32[4]{0:T(128)}, u32[]{:S(2)}) copy-start(s32[4]{0:T(128)} %param.11) | copy-start | bytes 52
  14.5 391.8 %all-to-all-start = ((bf16[32,128,2000]{1,2,0:T(8,128)(2,1)}), bf16[32,128,2000]{1,2,0:T(8,128)(2,1)}, u32[]{:S(2)}, u32[]{:S(2)}) async-start(bf16[32,128,2000]{1,2,0:T(8,128)(2,1)} %stack.2), calls=%async_computation | async-start | bytes 32768000 | tf_op jit(solution)/shard_map/all_to_all | solution.py:13
  26.8 645.0 %all-reduce.4.cloned.1.call-start = ((), (), s32[]{:S(2)}) async-start(), calls=%async_computation.3 | async-start | bytes 2097152
  27.6 401.2 %copy-start.12 = (f32[2000]{0:T(1024)S(1)}, f32[2000]{0:T(1024)}, u32[]{:S(2)}) copy-start(f32[2000]{0:T(1024)} %param.10) | copy-start | bytes 24004
  441.1 2.3 copy-start.2
  448.7 77.9 %copy-start.7 = (f32[4,8]{1,0:T(4,128)S(1)}, f32[4,8]{1,0:T(4,128)}, u32[]{:S(2)}) copy-start(f32[4,8]{1,0:T(4,128)} %param.15) | copy-start | bytes 388
  501.2 28.2 %copy-start.13 = (u32[256]{0:T(256)S(1)}, u32[256]{0:T(256)}, u32[]{:S(2)}) copy-start(u32[256]{0:T(256)} %constant.40) | copy-start | bytes 3076
  526.8 5.4 copy-start.6
  529.0 212.6 %reduce-scatter.2.cloned.1.call-start = ((), (), s32[]{:S(2)}) async-start(), calls=%async_computation.2 | async-start | bytes 7077888 | tf_op jit(solution)/shard_map/reduce_scatter | solution.py:68
  674.0 4.6 copy-start.3
  678.7 2.3 copy-start.4
  678.7 2.8 copy-start.5
  694.9 46.7 %copy-start.1 = (bf16[384,4096]{1,0:T(8,128)(2,1)S(1)}, bf16[384,4096]{1,0:T(8,128)(2,1)}, u32[]{:S(2)}) copy-start(bf16[384,4096]{1,0:T(8,128)(2,1)} %param.8) | copy-start | bytes 9437188
Sparse Core Ops, SparseCore 0:
  529.1 142.5 all-reduce.3
  695.1 46.4 reduce-scatter.1
